TPU v7x, 256 devices: a whole 4x4x8 slice. The times are simulated.
256 devices in a mesh: view: 16 (over z, x_hi), row: 4 (over x_lo, core), col: 4 (over y).
Axes of the slice: x: 4 (x_hi: 2, x_lo: 2; x = x_hi * 2 + x_lo), y: 4, z: 8, core: 2. Of those that a mesh axis runs over, the one named last changes fastest.
Arguments:
- residual: bfloat16 [16, 32, 128, 1024], P('view', 'row', 'col'), may hold values from -6 to 6
- window_query: bfloat16 [16, 32, 128, 1024], P('view', 'row', 'col'), may hold values from -56 to 56
- window_pairs: bfloat16 [2, 16, 32, 128, 1024], P(None, 'view', 'row', 'col'), may hold values from -4 to 4
- near_output: bfloat16 [1024, 1024], P('view'), may hold values from -0.1875 to 0.1875
- norm_gain: float32 [1024], replicated, may hold values from 0.1 to 1.9
- cross_input: bfloat16 [1024, 3072], P('view'), may hold values from -0.125 to 0.125
- head_gain: float32 [2, 64], replicated, may hold values from 0.7 to 6
- cross_output: bfloat16 [1024, 1024], P('view'), may hold values from -0.1875 to 0.1875
Outputs:
- block_out: bfloat16 [16, 32, 128, 1024], P('view', 'row', 'col')
All inputs are finite; a program needn't handle non-finite values.
Results may differ from a plain program's by a relative error of at most 0.018.
Values may be sent and summed in bfloat16 or wider, within the bound.
A program may use at most 128 MiB of HBM per device.

v0:
```python
import jax
import jax.numpy as jnp
from jax import lax
from jax.sharding import PartitionSpec as P

HEAD_DIM = 64
WINDOW = 13
RADIUS = 6


def padded(block, sides, width):
    for axis, dim in sides:
        count = lax.axis_size(axis)
        forward = [(i, i + 1) for i in range(count - 1)]
        backward = [(target, source) for source, target in forward]
        low = lax.ppermute(
            lax.slice_in_dim(block, block.shape[dim] - width, None, axis=dim), axis, forward
        )
        high = lax.ppermute(lax.slice_in_dim(block, 0, width, axis=dim), axis, backward)
        block = jnp.concatenate([low, block, high], axis=dim)
    return block


def window_mask(span_count, offset, total):
    queried = offset + jnp.arange(span_count, dtype=jnp.int32)
    keyed = offset - RADIUS + jnp.arange(span_count + 2 * RADIUS, dtype=jnp.int32)
    first_at = jnp.clip(queried - RADIUS, 0, total - WINDOW)
    return (keyed[None, :] >= first_at[:, None]) & (
        keyed[None, :] <= first_at[:, None] + WINDOW - 1
    )


def both_masks(tile_rows, tile_cols, row_start, col_start, row_count, col_count):
    by_row = window_mask(tile_rows, row_start, row_count)
    by_col = window_mask(tile_cols, col_start, col_count)
    joined = by_row[:, None, :, None] & by_col[None, :, None, :]
    return joined.reshape(
        tile_rows * tile_cols, (tile_rows + 2 * RADIUS) * (tile_cols + 2 * RADIUS)
    )


def neighborhood(queries, key_tile, value_tile, allowed):
    token_count = queries.shape[0] * queries.shape[1]
    span_total = key_tile.shape[0] * key_tile.shape[1]
    features = queries.shape[2]
    head_count = features // HEAD_DIM
    query_heads = queries.reshape(token_count, head_count, HEAD_DIM).transpose(1, 0, 2)
    key_heads = key_tile.reshape(span_total, head_count, HEAD_DIM).transpose(1, 0, 2)
    value_heads = value_tile.reshape(span_total, head_count, HEAD_DIM).transpose(1, 0, 2)

    def one_head(pieces):
        query_h, key_h, value_h = pieces
        scores = jnp.dot(query_h, key_h.T, preferred_element_type=jnp.float32) * HEAD_DIM ** (-0.5)
        scores = jnp.where(allowed, scores, -jnp.inf)
        highest = jnp.max(scores, axis=1, keepdims=True)
        exponent = jnp.exp(scores - highest)
        summed = jnp.sum(exponent, axis=1, keepdims=True)
        mixture = jnp.dot(
            exponent.astype(jnp.bfloat16), value_h, preferred_element_type=jnp.float32
        )
        return (mixture / summed).astype(jnp.bfloat16)

    result = lax.map(one_head, (query_heads, key_heads, value_heads))
    return result.transpose(1, 0, 2).reshape(token_count, features)


def rms_scale(values, gain_vec, epsilon):
    meansq = jnp.mean(values * values, axis=-1, keepdims=True)
    return values * lax.rsqrt(meansq + epsilon) * gain_vec


def split_projected(projected, head_gain, features):
    token_count = projected.shape[0]
    head_count = features // HEAD_DIM
    queried = rms_scale(
        projected[:, :features].reshape(token_count, head_count, HEAD_DIM), head_gain[0], 1e-06
    )
    keyed = rms_scale(
        projected[:, features : 2 * features].reshape(token_count, head_count, HEAD_DIM),
        head_gain[1],
        1e-06,
    )
    return (
        queried.astype(jnp.bfloat16).reshape(token_count, features),
        keyed.astype(jnp.bfloat16).reshape(token_count, features),
        projected[:, 2 * features :].astype(jnp.bfloat16),
    )


def across(queries, key_views, value_views):
    view_count, token_count, features = queries.shape
    other_count = key_views.shape[0]
    head_count = features // HEAD_DIM
    queried = queries.reshape(view_count, token_count, head_count, HEAD_DIM)
    keyed = key_views.reshape(other_count, token_count, head_count, HEAD_DIM)
    valued = value_views.reshape(other_count, token_count, head_count, HEAD_DIM)
    scores = jnp.einsum(
        "vnhd,wnhd->nhvw", queried, keyed, preferred_element_type=jnp.float32
    ) * HEAD_DIM ** (-0.5)
    highest = jnp.max(scores, axis=3, keepdims=True)
    exponent = jnp.exp(scores - highest)
    summed = jnp.sum(exponent, axis=3)
    mixture = jnp.einsum(
        "nhvw,wnhd->vnhd", exponent.astype(jnp.bfloat16), valued, preferred_element_type=jnp.float32
    )
    mixture = mixture / jnp.transpose(summed, (2, 0, 1))[..., None]
    return mixture.astype(jnp.bfloat16).reshape(view_count, token_count, features)


def row_folder(left_rows, piece):
    return jnp.dot(left_rows, piece, preferred_element_type=jnp.float32)


def attend_pixels(pieces):
    query_part, pair_part = pieces
    return across(query_part[0, :, 0], pair_part[0, :, 0], pair_part[1, :, 0])


def local(
    residual,
    window_query,
    window_pairs,
    near_output,
    norm_gain,
    cross_input,
    head_gain,
    cross_output,
):
    tile_rows = residual.shape[1]
    tile_cols = residual.shape[2]
    features = residual.shape[3]
    token_count = tile_rows * tile_cols
    groups = lax.axis_size("view")
    group_len = token_count // groups
    nearby = padded(window_pairs, (("row", 2), ("col", 3)), RADIUS)
    row_start = lax.axis_index("row") * tile_rows
    col_start = lax.axis_index("col") * tile_cols
    allowed = both_masks(
        tile_rows,
        tile_cols,
        row_start,
        col_start,
        tile_rows * lax.axis_size("row"),
        tile_cols * lax.axis_size("col"),
    )
    attended = neighborhood(window_query[0], nearby[0, 0], nearby[1, 0], allowed)
    near_term = row_folder(attended, lax.all_gather(near_output, "view", axis=0, tiled=True))
    residue = residual[0].reshape(token_count, features)
    hidden = (residue.astype(jnp.float32) + near_term).astype(jnp.bfloat16)
    normed = rms_scale(hidden.astype(jnp.float32), norm_gain, 1e-05).astype(jnp.bfloat16)
    projected = row_folder(normed, lax.all_gather(cross_input, "view", axis=0, tiled=True))
    queried, keyed, valued = split_projected(projected, head_gain, features)
    query_block = queried.reshape(1, 1, groups, group_len, features)
    pair_block = jnp.stack([keyed, valued]).reshape(2, 1, groups, group_len, features)
    mixture = attend_pixels(
        (
            lax.all_to_all(query_block, "view", split_axis=2, concat_axis=1, tiled=True),
            lax.all_to_all(pair_block, "view", split_axis=2, concat_axis=1, tiled=True),
        )
    )
    returned = lax.all_to_all(mixture, "view", split_axis=0, concat_axis=1, tiled=True)
    crossed = returned[0]
    cross_term = row_folder(crossed, lax.all_gather(cross_output, "view", axis=0, tiled=True))
    block_out = (hidden.astype(jnp.float32) + cross_term).astype(jnp.bfloat16)
    return block_out.reshape(1, tile_rows, tile_cols, features)


def solution(mesh):
    in_specs = (
        P("view", "row", "col", None),
        P("view", "row", "col", None),
        P(None, "view", "row", "col", None),
        P("view", None),
        P(),
        P("view", None),
        P(),
        P("view", None),
    )
    out_specs = P("view", "row", "col", None)
    return jax.shard_map(local, mesh=mesh, in_specs=in_specs, out_specs=out_specs, check_vma=False)
```

profile of v0, /device:TPU:8, one launch (start us, length us, event | category | flops | bytes accessed | tf_op | source)
XLA Modules:
  0.0 355.5 jit_solution(18072664135709869636)
XLA Ops:
  7.3 2.7 fusion.42
  10.0 1.8 collective-permute-start
  14.3 3.3 collective-permute-done.1
  19.1 1.7 pad_maximum_fusion.4
  20.8 3.5 collective-permute-start.2
  24.3 3.3 collective-permute-start.3
  27.6 2.5 reshape_squeeze.19
  30.1 2.5 copy.47
  32.9 3.5 collective-permute-done.3
  36.4 2.9 pad_maximum_fusion
  39.7 2.3 copy.45
  42.0 6.0 %reshape_squeeze.20 = bf16[880,16,64]{2,1,0:T(8,128)(2,1)} reshape(bf16[1,1,20,44,1024]{4,3,2,1,0:T(8,128)(2,1)} %copy.45) | data formatting | bytes 3604480 | tf_op jit(solution)/shard_map/reshape;squeeze | solution.py:48
  48.0 4.8 %copy.48 = bf16[16,880,64]{2,1,0:T(8,128)(2,1)} copy(bf16[16,880,64]{2,0,1:T(8,128)(2,1)} %bitcast.74) | data formatting | bytes 3604480
  52.8 2.3 copy.46
  55.1 5.9 %reshape_squeeze.21 = bf16[880,16,64]{2,1,0:T(8,128)(2,1)} reshape(bf16[1,1,20,44,1024]{4,3,2,1,0:T(8,128)(2,1)} %copy.46) | data formatting | bytes 3604480 | tf_op jit(solution)/shard_map/reshape;squeeze | solution.py:49
  61.0 5.0 %copy.49 = bf16[16,880,64]{2,1,0:T(8,128)(2,1)} copy(bf16[16,880,64]{2,0,1:T(8,128)(2,1)} %bitcast.75) | data formatting | bytes 3604480
  66.0 73.5 %while.11 = (s32[]{:T(128)}, bf16[16,256,64]{1,2,0:T(8,128)(2,1)S(1)}, bf16[16,256,64]{2,1,0:T(8,128)(2,1)}, bf16[16,880,64]{2,1,0:T(8,128)(2,1)}, bf16[16,880,6...) while((s32[]{:T(128)}, ...), condition=%wide.region_3.4_spmd.clone, body=%wide.region_0.3_spmd.clone.sunk | while | flops 59506176 | bytes 4612725 | solution.py:63
  139.6 2.4 fusion.23
  142.1 71.8 %all-gather.6.cloned.1.call-done = bf16[1024,3072]{1,0:T(8,128)(2,1)} async-done(((bf16[64,3072]{1,0:T(8,128)(2,1)}), bf16[1024,3072]{1,0:T(8,128)(2,1)}) %all-gather.6.cloned.1.call-update) | async-done | bytes 6291472 | tf_op jit(solution)/shard_map/all_gather | solution.py:151
  213.8 4.7 %fusion.34 = f32[256,3072]{1,0:T(8,128)S(1)} fusion(bf16[1024,3072]{1,0:T(8,128)(2,1)} %all-gather.6.cloned.1.call-done, bf16[256,1024]{1,0:T(8,128)(2,1)S(1)} %get-tuple-element.108, f32[1024]{0:T(1024)S(1)} %copy-done.10, f32[256]{0:T(256)S(1)} %add_rsqrt_fusion.2), kind=kOutput, calls=%fused_computation.52 | convolution fusion | flops 1611661312 | bytes 9966592 | tf_op jit(solution)/shard_map/dot_general | solution.py:111
  218.5 2.1 slice_multiply_fusion
  222.8 2.3 fusion.33
  225.1 4.6 %all-to-all-start.1 = ((bf16[1,1,16,16,1024]{4,3,1,0,2:T(8,128)(2,1)}), bf16[1,1,16,16,1024]{4,3,1,0,2:T(8,128)(2,1)}, u32[]{:S(2)}, u32[]{:S(2)}) async-start(bf16[1,1,16,16,1024]{4,3,1,0,2:T(8,128)(2,1)} %fusion.33), calls=%async_computation.1 | async-start | bytes 1048576 | tf_op jit(solution)/shard_map/all_to_all | solution.py:157
  229.8 2.1 slice.68
  236.3 11.7 %all-to-all-done.1 = bf16[1,1,16,16,1024]{4,3,1,0,2:T(8,128)(2,1)} async-done(((bf16[1,1,16,16,1024]{4,3,1,0,2:T(8,128)(2,1)}), bf16[1,1,16,16,1024]{4,3,1,0,2:T(8,128)(2,1)}, u32[]{:S(2)}, u32[]{:S(2)}) %all-to-all-start.1) | async-done | bytes 524320 | tf_op jit(solution)/shard_map/all_to_all | solution.py:157
  248.1 3.7 %all-to-all-start = ((bf16[2,1,16,16,1024]{4,3,1,0,2:T(8,128)(2,1)}), bf16[2,1,16,16,1024]{4,3,1,0,2:T(8,128)(2,1)S(1)}, u32[]{:S(2)}, u32[]{:S(2)}) async-start(bf16[2,1,16,16,1024]{4,3,1,0,2:T(8,128)(2,1)} %copy.52), calls=%async_computation | async-start | bytes 2097152 | tf_op jit(solution)/shard_map/all_to_all | solution.py:158
  252.5 2.0 reshape_squeeze.23
  254.5 24.7 %all-to-all-done = bf16[2,1,16,16,1024]{4,3,1,0,2:T(8,128)(2,1)S(1)} async-done(((bf16[2,1,16,16,1024]{4,3,1,0,2:T(8,128)(2,1)}), bf16[2,1,16,16,1024]{4,3,1,0,2:T(8,128)(2,1)S(1)}, u32[]{:S(2)}, u32[]{:S(2)}) %all-to-all-start) | async-done | bytes 1048608 | tf_op jit(solution)/shard_map/all_to_all | solution.py:158
  280.0 1.6 reshape_squeeze.22
  287.6 4.2 %all-to-all-start.2 = ((bf16[16,16,1024]{2,1,0:T(8,128)(2,1)}), bf16[16,16,1024]{2,1,0:T(8,128)(2,1)S(1)}, u32[]{:S(2)}, u32[]{:S(2)}) async-start(bf16[16,16,1024]{2,1,0:T(8,128)(2,1)} %reshape.267), calls=%async_computation.2 | async-start | bytes 1048576 | tf_op jit(solution)/shard_map/all_to_all | solution.py:161
  291.8 54.1 %all-gather.8.cloned.1.call-done = bf16[1024,1024]{1,0:T(8,128)(2,1)} async-done(((bf16[64,1024]{1,0:T(8,128)(2,1)}), bf16[1024,1024]{1,0:T(8,128)(2,1)}) %all-gather.8.cloned.1.call-update) | async-done | bytes 2097168 | tf_op jit(solution)/shard_map/all_gather | solution.py:163
  345.9 3.1 fusion.21
  (168 shorter events, 92.4 us)
Async XLA Ops:
  6.5 6.6 %copy-start = (bf16[2,1,8,32,1024]{4,3,2,1,0:T(8,128)(2,1)S(1)}, bf16[2,1,8,32,1024]{4,3,2,1,0:T(8,128)(2,1)}, u32[]{:S(2)}) copy-start(bf16[2,1,8,32,1024]{4,3,2,1,0:T(8,128)(2,1)} %param.12) | copy-start | bytes 3145732
  6.5 133.0 %all-gather.4.cloned.1.call-start = ((), (), s32[]{:S(2)}) async-start(), calls=%async_computation.3 | async-start | bytes 2228224 | tf_op jit(solution)/shard_map/all_gather | solution.py:147
  7.3 6.5 %copy-start.9 = (f32[2,64]{1,0:T(2,128)S(1)}, f32[2,64]{1,0:T(2,128)}, u32[]{:S(2)}) copy-start(f32[2,64]{1,0:T(2,128)} %param.16) | copy-start | bytes 1540
  7.3 206.5 %all-gather.6.cloned.1.call-start = ((), (), s32[]{:S(2)}) async-start(), calls=%async_computation.4 | async-start | bytes 6684672 | tf_op jit(solution)/shard_map/all_gather | solution.py:151
  10.0 3.8 %collective-permute-start = (bf16[2,1,6,32,1024]{4,3,2,1,0:T(8,128)(2,1)}, bf16[2,1,6,32,1024]{4,3,2,1,0:T(8,128)(2,1)S(1)}, u32[]{:S(2)}, u32[]{:S(2)}) collective-permute-start(bf16[2,1,6,32,1024]{4,3,2,1,0:T(8,128)(2,1)} %get-tuple-element.103), channel_id=1, source_target_pairs={{0,4},{4,8},{8,12},{1,5},{5,9},{9,13},{2,6},{6,10},{10,14},{3,7},{... | collective-permute-start | bytes 2359304 | tf_op jit(solution)/shard_map/ppermute | solution.py:16
  11.8 5.8 %collective-permute-start.1 = (bf16[2,1,6,32,1024]{4,3,2,1,0:T(8,128)(2,1)}, bf16[2,1,6,32,1024]{4,3,2,1,0:T(8,128)(2,1)}, u32[]{:S(2)}, u32[]{:S(2)}) collective-permute-start(bf16[2,1,6,32,1024]{4,3,2,1,0:T(8,128)(2,1)} %get-tuple-element.104), channel_id=1, source_target_pairs={{4,0},{8,4},{12,8},{5,1},{9,5},{13,9},{6,2},{10,6},{14,10},{7,3},{... | collective-permute-start | bytes 2359304 | tf_op jit(solution)/shard_map/ppermute | solution.py:19
  20.8 12.1 %collective-permute-start.2 = (bf16[2,1,20,6,1024]{4,2,3,1,0:T(8,128)(2,1)}, bf16[2,1,20,6,1024]{4,2,3,1,0:T(8,128)(2,1)}, u32[]{:S(2)}, u32[]{:S(2)}) collective-permute-start(bf16[2,1,20,6,1024]{4,2,3,1,0:T(8,128)(2,1)} %get-tuple-element.99), channel_id=1, source_target_pairs={{0,1},{1,2},{2,3},{4,5},{5,6},{6,7},{8,9},{9,10},{10,11},{12,13},{... | collective-permute-start | bytes 1474568 | tf_op jit(solution)/shard_map/ppermute | solution.py:16
  24.3 12.1 %collective-permute-start.3 = (bf16[2,1,20,6,1024]{4,2,3,1,0:T(8,128)(2,1)}, bf16[2,1,20,6,1024]{4,2,3,1,0:T(8,128)(2,1)}, u32[]{:S(2)}, u32[]{:S(2)}) collective-permute-start(bf16[2,1,20,6,1024]{4,2,3,1,0:T(8,128)(2,1)} %get-tuple-element.100), channel_id=1, source_target_pairs={{1,0},{2,1},{3,2},{5,4},{6,5},{7,6},{9,8},{10,9},{11,10},{13,12},{... | collective-permute-start | bytes 1474568 | tf_op jit(solution)/shard_map/ppermute | solution.py:19
  61.0 5.0 %copy-start.8 = (bf16[16,256,64]{1,2,0:T(8,128)(2,1)S(1)}, bf16[16,256,64]{1,2,0:T(8,128)(2,1)}, u32[]{:S(2)}) copy-start(bf16[16,256,64]{1,2,0:T(8,128)(2,1)} %custom-call) | copy-start | bytes 1572868
  66.0 73.6 %copy-start.5 = (bf16[1,8,32,1024]{3,2,1,0:T(8,128)(2,1)S(1)}, bf16[1,8,32,1024]{3,2,1,0:T(8,128)(2,1)}, u32[]{:S(2)}) copy-start(bf16[1,8,32,1024]{3,2,1,0:T(8,128)(2,1)} %param.10) | copy-start | bytes 1572868
  139.5 74.3 %copy-start.10 = (f32[1024]{0:T(1024)S(1)}, f32[1024]{0:T(1024)}, u32[]{:S(2)}) copy-start(f32[1024]{0:T(1024)} %param.14) | copy-start | bytes 12292
  142.0 76.4 %copy-start.6 = (bf16[256,1024]{1,0:T(8,128)(2,1)}, bf16[256,1024]{1,0:T(8,128)(2,1)S(1)}, u32[]{:S(2)}) copy-start(bf16[256,1024]{1,0:T(8,128)(2,1)S(1)} %get-tuple-element.108) | copy-start | bytes 1572868
  218.5 2.6 copy-start.2
  222.8 9.1 %copy-start.1 = (f32[256,1024]{1,0:T(8,128)S(1)}, f32[256,1024]{1,0:T(8,128)}, u32[]{:S(2)}) copy-start(f32[256,1024]{1,0:T(8,128)} %get-tuple-element.96) | copy-start | bytes 3145732
  225.1 22.9 %all-to-all-start.1 = ((bf16[1,1,16,16,1024]{4,3,1,0,2:T(8,128)(2,1)}), bf16[1,1,16,16,1024]{4,3,1,0,2:T(8,128)(2,1)}, u32[]{:S(2)}, u32[]{:S(2)}) async-start(bf16[1,1,16,16,1024]{4,3,1,0,2:T(8,128)(2,1)} %fusion.33), calls=%async_computation.1 | async-start | bytes 1048576 | tf_op jit(solution)/shard_map/all_to_all | solution.py:157
  233.7 1.5 copy-start.3
  248.1 31.2 %all-to-all-start = ((bf16[2,1,16,16,1024]{4,3,1,0,2:T(8,128)(2,1)}), bf16[2,1,16,16,1024]{4,3,1,0,2:T(8,128)(2,1)S(1)}, u32[]{:S(2)}, u32[]{:S(2)}) async-start(bf16[2,1,16,16,1024]{4,3,1,0,2:T(8,128)(2,1)} %copy.52), calls=%async_computation | async-start | bytes 2097152 | tf_op jit(solution)/shard_map/all_to_all | solution.py:158
  251.7 94.2 %all-gather.8.cloned.1.call-start = ((), (), s32[]{:S(2)}) async-start(), calls=%async_computation.5 | async-start | bytes 2228224 | tf_op jit(solution)/shard_map/all_gather | solution.py:163
  283.2 1.2 copy-start.4
  285.8 60.1 %copy-start.7 = (bf16[256,1024]{1,0:T(8,128)(2,1)S(1)}, bf16[256,1024]{1,0:T(8,128)(2,1)}, u32[]{:S(2)}) copy-start(bf16[256,1024]{1,0:T(8,128)(2,1)} %copy-done.6) | copy-start | bytes 1572868
  287.6 58.3 %all-to-all-start.2 = ((bf16[16,16,1024]{2,1,0:T(8,128)(2,1)}), bf16[16,16,1024]{2,1,0:T(8,128)(2,1)S(1)}, u32[]{:S(2)}, u32[]{:S(2)}) async-start(bf16[16,16,1024]{2,1,0:T(8,128)(2,1)} %reshape.267), calls=%async_computation.2 | async-start | bytes 1048576 | tf_op jit(solution)/shard_map/all_to_all | solution.py:161
Sparse Core Ops, SparseCore 0:
  9.9 88.6 all-gather.3
  101.3 112.5 all-gather.5
  255.1 90.7 all-gather.7
where the time goes:
time: 357 us; the launch traced here: 356 us
  waiting for transfers between devices  171 us (48%)
  local copies, waits for them, and re-layouts  72.7 us (20%)
  matrix products  53.9 us (15%)
  starting transfers between devices  22.4 us (6%)
  other arithmetic  21.7 us (6%)
  between operations  13.5 us (4%)
    all_gather x1, waiting for transfers between devices, local(): lax.all_gather(cross_input, 'view', axis=0, tiled=True)  71.8 us
    all_gather x1, waiting for transfers between devices, local(): lax.all_gather(cross_output, 'view', axis=0, tiled=True)  54.1 us
    all_to_all x1, waiting for transfers between devices, local(): lax.all_to_all(pair_block, 'view', split_axis=2, concat_axis=1, tiled=True)  24.7 us
    and x32, local copies, waits for them, and re-layouts, both_masks(): joined = by_row[:, None, :, None] & by_col[None, :, None, :]  22 us
    dot_general x16, matrix products, one_head(): jnp.dot(query_h, key_h.T, preferred_element_type=jnp.float32)  21.1 us
    dot_general x16, matrix products, one_head(): jnp.dot(exponent.astype(jnp.bfloat16), value_h, preferred_element_type=jn...  19.7 us
    unnamed x26, local copies, waits for them, and re-layouts  13.8 us
    all_to_all x1, waiting for transfers between devices, local(): lax.all_to_all(query_block, 'view', split_axis=2, concat_axis=1, tiled=True)  11.7 us
  transfers between devices with their start and end apart: 10, of which 7 were waited for; matrix products, arithmetic and copies ran while one was open for 38% of the time, Pallas kernels for 0%

commit v1 on v0

--- a/solution.py
+++ b/solution.py
@@ -6,6 +6,13 @@
 HEAD_DIM = 64
 WINDOW = 13
 RADIUS = 6
+
+
+def exchange_gather(array, axis, d):
+    count = lax.axis_size(axis)
+    pieces = jnp.stack([array for _ in range(count)])
+    pieces = lax.all_to_all(pieces, axis, split_axis=0, concat_axis=0)
+    return jnp.concatenate(pieces, axis=d)
 
 
 def padded(block, sides, width):
@@ -148,7 +155,7 @@
     residue = residual[0].reshape(token_count, features)
     hidden = (residue.astype(jnp.float32) + near_term).astype(jnp.bfloat16)
     normed = rms_scale(hidden.astype(jnp.float32), norm_gain, 1e-05).astype(jnp.bfloat16)
-    projected = row_folder(normed, lax.all_gather(cross_input, "view", axis=0, tiled=True))
+    projected = row_folder(normed, exchange_gather(cross_input, "view", 0))
     queried, keyed, valued = split_projected(projected, head_gain, features)
     query_block = queried.reshape(1, 1, groups, group_len, features)
     pair_block = jnp.stack([keyed, valued]).reshape(2, 1, groups, group_len, features)

time: 357 us -> 334 us (0.936)
  waiting for transfers between devices: 171 us -> 131 us
  starting transfers between devices: 22.4 us -> 34.4 us
    all_gather x1 -> x0, waiting for transfers between devices: 71.8 us -> none  [local(): lax.all_gather(cross_input, 'view', axis=0, tiled=True)]
    all_gather x1, waiting for transfers between devices: 0.02 us -> 30.1 us  [local(): lax.all_gather(near_output, 'view', axis=0, tiled=True)]
    all_to_all x0 -> x1, starting transfers between devices: none -> 11.2 us  [exchange_gather(): pieces = lax.all_to_all(pieces, axis, split_axis=0, concat_axis=0)]
    ppermute x2, waiting for transfers between devices: 0.11 us -> 5.53 us  [padded(): lax.ppermute(lax.slice_in_dim(block, block.shape[dim] - width, None, axis...]
    unnamed x26 -> x28, local copies, waits for them, and re-layouts: 13.8 us -> 13.6 us
  transfers between devices with their start and end apart: 10 -> 10, of which waited for: 7 -> 6; matrix products, arithmetic and copies ran while one was open for 38% -> 40% of each run, Pallas kernels for 0% -> 0%
where the time goes in v1:
time: 334 us; the launch traced here: 332 us
  waiting for transfers between devices  131 us (39%)
  local copies, waits for them, and re-layouts  75.9 us (23%)
  matrix products  54.1 us (16%)
  starting transfers between devices  34.4 us (10%)
  other arithmetic  21.6 us (6%)
  between operations  13.8 us (4%)
    all_gather x1, waiting for transfers between devices, local(): lax.all_gather(cross_output, 'view', axis=0, tiled=True)  53.2 us
    all_gather x1, waiting for transfers between devices, local(): lax.all_gather(near_output, 'view', axis=0, tiled=True)  30.1 us
    all_to_all x1, waiting for transfers between devices, local(): lax.all_to_all(pair_block, 'view', split_axis=2, concat_axis=1, tiled=True)  26.3 us
    and x32, local copies, waits for them, and re-layouts, both_masks(): joined = by_row[:, None, :, None] & by_col[None, :, None, :]  22 us
    dot_general x16, matrix products, one_head(): jnp.dot(query_h, key_h.T, preferred_element_type=jnp.float32)  21 us
    dot_general x16, matrix products, one_head(): jnp.dot(exponent.astype(jnp.bfloat16), value_h, preferred_element_type=jn...  19.7 us
    unnamed x28, local copies, waits for them, and re-layouts  13.6 us
    all_to_all x1, waiting for transfers between devices, local(): lax.all_to_all(query_block, 'view', split_axis=2, concat_axis=1, tiled=True)  11.6 us
  transfers between devices with their start and end apart: 10, of which 6 were waited for; matrix products, arithmetic and copies ran while one was open for 40% of the time, Pallas kernels for 0%

profile of v1, /device:TPU:8, one launch (start us, length us, event | category | flops | bytes accessed | tf_op | source)
XLA Modules:
  0.0 331.7 jit_solution(7150141769788678404)
XLA Ops:
  6.5 2.8 fusion.42
  9.3 1.8 collective-permute-start
  12.4 3.4 %stack.6 = bf16[16,64,3072]{2,1,0:T(8,128)(2,1)} broadcast(bf16[64,3072]{1,0:T(8,128)(2,1)S(1)} %copy-done.9), dimensions={1,2} | broadcast | bytes 6684672 | tf_op jit(solution)/shard_map/stack | solution.py:13
  15.8 11.2 %all-to-all-start = ((bf16[16,64,3072]{2,1,0:T(8,128)(2,1)}), bf16[16,64,3072]{2,1,0:T(8,128)(2,1)}, u32[]{:S(2)}, u32[]{:S(2)}) async-start(bf16[16,64,3072]{2,1,0:T(8,128)(2,1)} %stack.6), calls=%async_computation | async-start | bytes 12582912 | tf_op jit(solution)/shard_map/all_to_all | solution.py:14
  31.3 3.5 %collective-permute-start.2 = (bf16[2,1,20,6,1024]{4,2,3,1,0:T(8,128)(2,1)}, bf16[2,1,20,6,1024]{4,2,3,1,0:T(8,128)(2,1)}, u32[]{:S(2)}, u32[]{:S(2)}) collective-permute-start(bf16[2,1,20,6,1024]{4,2,3,1,0:T(8,128)(2,1)} %get-tuple-element.99), channel_id=1, source_target_pairs={{0,1},{1,2},{2,3},{4,5},{5,6},{6,7},{8,9},{9,10},{10,11},{12,13},{... | collective-permute-start | bytes 1474568 | tf_op jit(solution)/shard_map/ppermute | solution.py:23
  34.8 3.3 %collective-permute-start.3 = (bf16[2,1,20,6,1024]{4,2,3,1,0:T(8,128)(2,1)}, bf16[2,1,20,6,1024]{4,2,3,1,0:T(8,128)(2,1)}, u32[]{:S(2)}, u32[]{:S(2)}) collective-permute-start(bf16[2,1,20,6,1024]{4,2,3,1,0:T(8,128)(2,1)} %get-tuple-element.100), channel_id=1, source_target_pairs={{1,0},{2,1},{3,2},{5,4},{6,5},{7,6},{9,8},{10,9},{11,10},{13,12},{... | collective-permute-start | bytes 1474568 | tf_op jit(solution)/shard_map/ppermute | solution.py:26
  38.2 2.5 reshape_squeeze.19
  40.7 2.5 copy.47
  43.4 5.5 %collective-permute-done.2 = bf16[2,1,20,6,1024]{4,2,3,1,0:T(8,128)(2,1)} collective-permute-done((bf16[2,1,20,6,1024]{4,2,3,1,0:T(8,128)(2,1)}, bf16[2,1,20,6,1024]{4,2,3,1,0:T(8,128)(2,1)}, u32[]{:S(2)}, u32[]{:S(2)}) %collective-permute-start.2) | collective-permute-done | bytes 491552 | tf_op jit(solution)/shard_map/ppermute | solution.py:23
  49.0 3.8 %collective-permute-done.3 = bf16[2,1,20,6,1024]{4,2,3,1,0:T(8,128)(2,1)} collective-permute-done((bf16[2,1,20,6,1024]{4,2,3,1,0:T(8,128)(2,1)}, bf16[2,1,20,6,1024]{4,2,3,1,0:T(8,128)(2,1)}, u32[]{:S(2)}, u32[]{:S(2)}) %collective-permute-start.3) | collective-permute-done | bytes 491552 | tf_op jit(solution)/shard_map/ppermute | solution.py:26
  52.8 2.9 pad_maximum_fusion
  56.1 2.3 copy.45
  58.4 5.9 %reshape_squeeze.20 = bf16[880,16,64]{2,1,0:T(8,128)(2,1)} reshape(bf16[1,1,20,44,1024]{4,3,2,1,0:T(8,128)(2,1)} %copy.45) | data formatting | bytes 3604480 | tf_op jit(solution)/shard_map/reshape;squeeze | solution.py:55
  64.3 4.7 %copy.48 = bf16[16,880,64]{2,1,0:T(8,128)(2,1)} copy(bf16[16,880,64]{2,0,1:T(8,128)(2,1)} %bitcast.75) | data formatting | bytes 3604480
  69.1 2.3 copy.46
  71.3 5.9 %reshape_squeeze.21 = bf16[880,16,64]{2,1,0:T(8,128)(2,1)} reshape(bf16[1,1,20,44,1024]{4,3,2,1,0:T(8,128)(2,1)} %copy.46) | data formatting | bytes 3604480 | tf_op jit(solution)/shard_map/reshape;squeeze | solution.py:56
  77.3 4.8 %copy.49 = bf16[16,880,64]{2,1,0:T(8,128)(2,1)} copy(bf16[16,880,64]{2,0,1:T(8,128)(2,1)} %bitcast.76) | data formatting | bytes 3604480
  82.1 73.5 %while.11 = (s32[]{:T(128)}, bf16[16,256,64]{1,2,0:T(8,128)(2,1)S(1)}, bf16[16,256,64]{2,1,0:T(8,128)(2,1)}, bf16[16,880,64]{2,1,0:T(8,128)(2,1)}, bf16[16,880,6...) while((s32[]{:T(128)}, ...), condition=%wide.region_3.4_spmd.clone, body=%wide.region_0.3_spmd.clone.sunk | while | flops 59506176 | bytes 4612725 | solution.py:70
  155.6 30.1 %all-gather.3.cloned.1.call-done = bf16[1024,1024]{1,0:T(8,128)(2,1)} async-done(((bf16[64,1024]{1,0:T(8,128)(2,1)}), bf16[1024,1024]{1,0:T(8,128)(2,1)}) %all-gather.3.cloned.1.call-update) | async-done | bytes 2097168 | tf_op jit(solution)/shard_map/all_gather | solution.py:154
  185.6 2.4 fusion.23
  188.1 4.8 %fusion.34 = f32[256,3072]{1,0:T(8,128)S(1)} fusion(bf16[1024,3072]{1,0:T(8,128)(2,1)} %bitcast.6, bf16[256,1024]{1,0:T(8,128)(2,1)S(1)} %get-tuple-element.108, f32[1024]{0:T(1024)S(1)} %copy-done.11, f32[256]{0:T(256)S(1)} %add_rsqrt_fusion.2), kind=kOutput, calls=%fused_computation.52 | convolution fusion | flops 1611661312 | bytes 9966592 | tf_op jit(solution)/shard_map/dot_general | solution.py:118
  193.0 2.1 slice_multiply_fusion
  197.3 2.3 fusion.33
  199.6 6.0 %all-to-all-start.2 = ((bf16[1,1,16,16,1024]{4,3,1,0,2:T(8,128)(2,1)}), bf16[1,1,16,16,1024]{4,3,1,0,2:T(8,128)(2,1)}, u32[]{:S(2)}, u32[]{:S(2)}) async-start(bf16[1,1,16,16,1024]{4,3,1,0,2:T(8,128)(2,1)} %fusion.33), calls=%async_computation.2 | async-start | bytes 1048576 | tf_op jit(solution)/shard_map/all_to_all | solution.py:164
  205.7 2.1 slice.68
  212.2 11.6 %all-to-all-done.2 = bf16[1,1,16,16,1024]{4,3,1,0,2:T(8,128)(2,1)} async-done(((bf16[1,1,16,16,1024]{4,3,1,0,2:T(8,128)(2,1)}), bf16[1,1,16,16,1024]{4,3,1,0,2:T(8,128)(2,1)}, u32[]{:S(2)}, u32[]{:S(2)}) %all-to-all-start.2) | async-done | bytes 524320 | tf_op jit(solution)/shard_map/all_to_all | solution.py:164
  223.8 3.7 %all-to-all-start.1 = ((bf16[2,1,16,16,1024]{4,3,1,0,2:T(8,128)(2,1)}), bf16[2,1,16,16,1024]{4,3,1,0,2:T(8,128)(2,1)S(1)}, u32[]{:S(2)}, u32[]{:S(2)}) async-start(bf16[2,1,16,16,1024]{4,3,1,0,2:T(8,128)(2,1)} %copy.52), calls=%async_computation.1 | async-start | bytes 2097152 | tf_op jit(solution)/shard_map/all_to_all | solution.py:165
  228.2 2.0 reshape_squeeze.23
  230.3 26.3 %all-to-all-done.1 = bf16[2,1,16,16,1024]{4,3,1,0,2:T(8,128)(2,1)S(1)} async-done(((bf16[2,1,16,16,1024]{4,3,1,0,2:T(8,128)(2,1)}), bf16[2,1,16,16,1024]{4,3,1,0,2:T(8,128)(2,1)S(1)}, u32[]{:S(2)}, u32[]{:S(2)}) %all-to-all-start.1) | async-done | bytes 1048608 | tf_op jit(solution)/shard_map/all_to_all | solution.py:165
  265.0 3.6 %all-to-all-start.3 = ((bf16[16,16,1024]{2,1,0:T(8,128)(2,1)}), bf16[16,16,1024]{2,1,0:T(8,128)(2,1)S(1)}, u32[]{:S(2)}, u32[]{:S(2)}) async-start(bf16[16,16,1024]{2,1,0:T(8,128)(2,1)} %reshape.273), calls=%async_computation.3 | async-start | bytes 1048576 | tf_op jit(solution)/shard_map/all_to_all | solution.py:168
  268.6 53.2 %all-gather.5.cloned.1.call-done = bf16[1024,1024]{1,0:T(8,128)(2,1)} async-done(((bf16[64,1024]{1,0:T(8,128)(2,1)}), bf16[1024,1024]{1,0:T(8,128)(2,1)}) %all-gather.5.cloned.1.call-update) | async-done | bytes 2097168 | tf_op jit(solution)/shard_map/all_gather | solution.py:170
  321.8 3.1 fusion.21
  (170 shorter events, 94.7 us)
Async XLA Ops:
  6.5 5.9 %copy-start.9 = (bf16[64,3072]{1,0:T(8,128)(2,1)S(1)}, bf16[64,3072]{1,0:T(8,128)(2,1)}, u32[]{:S(2)}) copy-start(bf16[64,3072]{1,0:T(8,128)(2,1)} %param.15) | copy-start | bytes 1179652
  6.5 179.1 %all-gather.3.cloned.1.call-start = ((), (), s32[]{:S(2)}) async-start(), calls=%async_computation.4 | async-start | bytes 2228224 | tf_op jit(solution)/shard_map/all_gather | solution.py:154
  9.3 18.4 %collective-permute-start = (bf16[2,1,6,32,1024]{4,3,2,1,0:T(8,128)(2,1)}, bf16[2,1,6,32,1024]{4,3,2,1,0:T(8,128)(2,1)S(1)}, u32[]{:S(2)}, u32[]{:S(2)}) collective-permute-start(bf16[2,1,6,32,1024]{4,3,2,1,0:T(8,128)(2,1)} %get-tuple-element.103), channel_id=1, source_target_pairs={{0,4},{4,8},{8,12},{1,5},{5,9},{9,13},{2,6},{6,10},{10,14},{3,7},{... | collective-permute-start | bytes 2359304 | tf_op jit(solution)/shard_map/ppermute | solution.py:23
  11.1 17.1 %collective-permute-start.1 = (bf16[2,1,6,32,1024]{4,3,2,1,0:T(8,128)(2,1)}, bf16[2,1,6,32,1024]{4,3,2,1,0:T(8,128)(2,1)}, u32[]{:S(2)}, u32[]{:S(2)}) collective-permute-start(bf16[2,1,6,32,1024]{4,3,2,1,0:T(8,128)(2,1)} %get-tuple-element.104), channel_id=1, source_target_pairs={{4,0},{8,4},{12,8},{5,1},{9,5},{13,9},{6,2},{10,6},{14,10},{7,3},{... | collective-permute-start | bytes 2359304 | tf_op jit(solution)/shard_map/ppermute | solution.py:26
  15.8 11.2 %copy-start = (bf16[2,1,8,32,1024]{4,3,2,1,0:T(8,128)(2,1)S(1)}, bf16[2,1,8,32,1024]{4,3,2,1,0:T(8,128)(2,1)}, u32[]{:S(2)}) copy-start(bf16[2,1,8,32,1024]{4,3,2,1,0:T(8,128)(2,1)} %param.12) | copy-start | bytes 3145732
  15.8 172.3 %all-to-all-start = ((bf16[16,64,3072]{2,1,0:T(8,128)(2,1)}), bf16[16,64,3072]{2,1,0:T(8,128)(2,1)}, u32[]{:S(2)}, u32[]{:S(2)}) async-start(bf16[16,64,3072]{2,1,0:T(8,128)(2,1)} %stack.6), calls=%async_computation | async-start | bytes 12582912 | tf_op jit(solution)/shard_map/all_to_all | solution.py:14
  27.1 0.7 copy-start.10
  31.3 17.6 %collective-permute-start.2 = (bf16[2,1,20,6,1024]{4,2,3,1,0:T(8,128)(2,1)}, bf16[2,1,20,6,1024]{4,2,3,1,0:T(8,128)(2,1)}, u32[]{:S(2)}, u32[]{:S(2)}) collective-permute-start(bf16[2,1,20,6,1024]{4,2,3,1,0:T(8,128)(2,1)} %get-tuple-element.99), channel_id=1, source_target_pairs={{0,1},{1,2},{2,3},{4,5},{5,6},{6,7},{8,9},{9,10},{10,11},{12,13},{... | collective-permute-start | bytes 1474568 | tf_op jit(solution)/shard_map/ppermute | solution.py:23
  34.8 17.9 %collective-permute-start.3 = (bf16[2,1,20,6,1024]{4,2,3,1,0:T(8,128)(2,1)}, bf16[2,1,20,6,1024]{4,2,3,1,0:T(8,128)(2,1)}, u32[]{:S(2)}, u32[]{:S(2)}) collective-permute-start(bf16[2,1,20,6,1024]{4,2,3,1,0:T(8,128)(2,1)} %get-tuple-element.100), channel_id=1, source_target_pairs={{1,0},{2,1},{3,2},{5,4},{6,5},{7,6},{9,8},{10,9},{11,10},{13,12},{... | collective-permute-start | bytes 1474568 | tf_op jit(solution)/shard_map/ppermute | solution.py:26
  77.3 4.8 %copy-start.8 = (bf16[16,256,64]{1,2,0:T(8,128)(2,1)S(1)}, bf16[16,256,64]{1,2,0:T(8,128)(2,1)}, u32[]{:S(2)}) copy-start(bf16[16,256,64]{1,2,0:T(8,128)(2,1)} %custom-call) | copy-start | bytes 1572868
  82.1 103.6 %copy-start.5 = (bf16[1,8,32,1024]{3,2,1,0:T(8,128)(2,1)S(1)}, bf16[1,8,32,1024]{3,2,1,0:T(8,128)(2,1)}, u32[]{:S(2)}) copy-start(bf16[1,8,32,1024]{3,2,1,0:T(8,128)(2,1)} %param.10) | copy-start | bytes 1572868
  155.6 32.5 %copy-start.11 = (f32[1024]{0:T(1024)S(1)}, f32[1024]{0:T(1024)}, u32[]{:S(2)}) copy-start(f32[1024]{0:T(1024)} %param.14) | copy-start | bytes 12292
  188.1 4.9 %copy-start.6 = (bf16[256,1024]{1,0:T(8,128)(2,1)}, bf16[256,1024]{1,0:T(8,128)(2,1)S(1)}, u32[]{:S(2)}) copy-start(bf16[256,1024]{1,0:T(8,128)(2,1)S(1)} %get-tuple-element.108) | copy-start | bytes 1572868
  193.0 2.6 copy-start.2
  197.3 10.5 %copy-start.1 = (f32[256,1024]{1,0:T(8,128)S(1)}, f32[256,1024]{1,0:T(8,128)}, u32[]{:S(2)}) copy-start(f32[256,1024]{1,0:T(8,128)} %get-tuple-element.96) | copy-start | bytes 3145732
  199.6 24.2 %all-to-all-start.2 = ((bf16[1,1,16,16,1024]{4,3,1,0,2:T(8,128)(2,1)}), bf16[1,1,16,16,1024]{4,3,1,0,2:T(8,128)(2,1)}, u32[]{:S(2)}, u32[]{:S(2)}) async-start(bf16[1,1,16,16,1024]{4,3,1,0,2:T(8,128)(2,1)} %fusion.33), calls=%async_computation.2 | async-start | bytes 1048576 | tf_op jit(solution)/shard_map/all_to_all | solution.py:164
  209.6 1.5 copy-start.3
  223.8 32.7 %all-to-all-start.1 = ((bf16[2,1,16,16,1024]{4,3,1,0,2:T(8,128)(2,1)}), bf16[2,1,16,16,1024]{4,3,1,0,2:T(8,128)(2,1)S(1)}, u32[]{:S(2)}, u32[]{:S(2)}) async-start(bf16[2,1,16,16,1024]{4,3,1,0,2:T(8,128)(2,1)} %copy.52), calls=%async_computation.1 | async-start | bytes 2097152 | tf_op jit(solution)/shard_map/all_to_all | solution.py:165
  227.5 94.2 %all-gather.5.cloned.1.call-start = ((), (), s32[]{:S(2)}) async-start(), calls=%async_computation.5 | async-start | bytes 2228224 | tf_op jit(solution)/shard_map/all_gather | solution.py:170
  260.5 1.2 copy-start.4
  263.2 58.6 %copy-start.7 = (bf16[256,1024]{1,0:T(8,128)(2,1)S(1)}, bf16[256,1024]{1,0:T(8,128)(2,1)}, u32[]{:S(2)}) copy-start(bf16[256,1024]{1,0:T(8,128)(2,1)} %copy-done.6) | copy-start | bytes 1572868
  265.0 56.8 %all-to-all-start.3 = ((bf16[16,16,1024]{2,1,0:T(8,128)(2,1)}), bf16[16,16,1024]{2,1,0:T(8,128)(2,1)S(1)}, u32[]{:S(2)}, u32[]{:S(2)}) async-start(bf16[16,16,1024]{2,1,0:T(8,128)(2,1)} %reshape.273), calls=%async_computation.3 | async-start | bytes 1048576 | tf_op jit(solution)/shard_map/all_to_all | solution.py:168
Sparse Core Ops, SparseCore 0:
  12.6 173.0 all-gather.2
  230.9 90.7 all-gather.4
